TPU v7x, 256 devices: a whole 4x4x8 slice. The times are simulated.
256 devices in a mesh: member: 16 (over z, y_hi), lat: 4 (over x), lon: 4 (over y_lo, core).
Axes of the slice: x: 4, y: 4 (y_hi: 2, y_lo: 2; y = y_hi * 2 + y_lo), z: 8, core: 2. Of those that a mesh axis runs over, the one named last changes fastest.
Arguments:
- ensemble: bfloat16 [32, 16, 64, 256], P('member', 'lat', 'lon'), may hold values from -12 to 12
- norm_gain: float32 [256], replicated, may hold values from 0.5 to 1.5
- project_weight: bfloat16 [256, 768], replicated, may hold values from -0.375 to 0.375
- output_weight: bfloat16 [256, 256], replicated, may hold values from -0.375 to 0.375
- conv_kernel: bfloat16 [3, 3, 256, 256], replicated, may hold values from -0.125 to 0.125
- cotangent: bfloat16 [32, 16, 64, 256], P('member', 'lat', 'lon'), may hold values from -6 to 6
Outputs:
- result: bfloat16 [32, 16, 64, 256], P('member', 'lat', 'lon')
- grad_ensemble: bfloat16 [32, 16, 64, 256], P('member', 'lat', 'lon')
All inputs are finite; a program needn't handle non-finite values.
Results may differ from a plain program's by a relative error of at most 0.018.
Values may be sent and summed in bfloat16 or wider, within the bound.
A program may use at most 64 MiB of HBM per device.

v0:
```python
import math
import jax
import jax.numpy as jnp
from jax import lax
from jax.sharding import PartitionSpec as P

HEAD_COUNT = 8
FLOOR = 0.5
EPSILON = 1e-06


def padded_2(block, sides, width, periodic):
    for axis, dim in sides:
        count = lax.axis_size(axis)
        forward = [(i, i + 1) for i in range(count - 1)]
        if periodic:
            forward.append((count - 1, 0))
        backward = [(target, source) for source, target in forward]
        low = lax.ppermute(
            lax.slice_in_dim(block, block.shape[dim] - width, None, axis=dim), axis, forward
        )
        high = lax.ppermute(lax.slice_in_dim(block, 0, width, axis=dim), axis, backward)
        block = jnp.concatenate([low, block, high], axis=dim)
    return block


def row_norm(values, gain_vec):
    mean_sq = jnp.mean(values * values, axis=-1, keepdims=True)
    return values * lax.rsqrt(mean_sq + EPSILON) * gain_vec


def head_norm(values, head_count):
    shaped = values.reshape(values.shape[:-1] + (head_count, values.shape[-1] // head_count))
    mean_sq = jnp.mean(shaped * shaped, axis=-1, keepdims=True)
    return (shaped * lax.rsqrt(jnp.maximum(mean_sq, FLOOR))).reshape(values.shape)


def split_heads(values, head_count):
    return values.reshape(values.shape[:-1] + (head_count, values.shape[-1] // head_count))


def head_pullback(raw_rows, grad_rows):
    _, pullback = jax.vjp(lambda t: head_norm(t, HEAD_COUNT), raw_rows.astype(jnp.float32))
    return pullback(grad_rows)[0]


def pad_field(field_in):
    widened = padded_2(field_in, (("lon", 2),), 1, True)
    return padded_2(widened, (("lat", 1),), 1, False)


def conv_taps(padded, kernel, lat_n, lon_n, adjoint):
    running = None
    for row_off in range(3):
        for col_off in range(3):
            if adjoint:
                window = padded[
                    :, 2 - row_off : 2 - row_off + lat_n, 2 - col_off : 2 - col_off + lon_n
                ]
                summand = jnp.einsum(
                    "mabc,dc->mabd",
                    window,
                    kernel[row_off, col_off],
                    preferred_element_type=jnp.float32,
                )
            else:
                window = padded[:, row_off : row_off + lat_n, col_off : col_off + lon_n]
                summand = jnp.einsum(
                    "mabc,cd->mabd",
                    window,
                    kernel[row_off, col_off],
                    preferred_element_type=jnp.float32,
                )
            running = summand if running is None else running + summand
    return running


def per_device(ensemble, norm_gain, project_weight, output_weight, conv_kernel, cotangent):
    mem_dev, lat_dev, lon_dev, channels = ensemble.shape
    cell_count = lat_dev * lon_dev
    score_scale = 1.0 / math.sqrt(channels // HEAD_COUNT)
    inputs = ensemble.reshape(mem_dev, cell_count, channels).astype(jnp.float32)
    normed = row_norm(inputs, norm_gain).astype(jnp.bfloat16)
    query_raw = jnp.dot(
        normed, project_weight[:, :channels], preferred_element_type=jnp.float32
    ).astype(jnp.bfloat16)
    gathered = jnp.dot(
        lax.all_gather(normed, "member", axis=0, tiled=True),
        project_weight[:, channels:],
        preferred_element_type=jnp.float32,
    ).astype(jnp.bfloat16)
    own_rows = lax.dynamic_slice_in_dim(gathered, lax.axis_index("member") * mem_dev, mem_dev, 0)
    key_raw = own_rows[..., :channels]
    key_rows = head_norm(gathered[..., :channels].astype(jnp.float32), HEAD_COUNT).astype(
        jnp.bfloat16
    )
    value_rows = gathered[..., channels:]
    queries = head_norm(query_raw.astype(jnp.float32), HEAD_COUNT).astype(jnp.bfloat16)
    query_heads = split_heads(queries, HEAD_COUNT)
    key_heads = split_heads(key_rows, HEAD_COUNT)
    value_heads = split_heads(value_rows, HEAD_COUNT)
    scores = (
        jnp.einsum("mphd,nphd->mnhp", query_heads, key_heads, preferred_element_type=jnp.float32)
        * score_scale
    )
    expd = jnp.exp(scores)
    soft = expd / jnp.sum(expd, axis=1, keepdims=True)
    rounded = soft.astype(jnp.bfloat16)
    mixed_out = jnp.einsum(
        "mnhp,nphd->mphd", rounded, value_heads, preferred_element_type=jnp.float32
    )
    mixed_out = mixed_out.reshape(query_raw.shape).astype(jnp.bfloat16)
    updated = (
        inputs + jnp.dot(mixed_out, output_weight, preferred_element_type=jnp.float32)
    ).astype(jnp.bfloat16)
    field_up = updated.reshape(mem_dev, lat_dev, lon_dev, channels)
    result = field_up.astype(jnp.float32) + conv_taps(
        pad_field(field_up), conv_kernel, lat_dev, lon_dev, False
    )
    result = result.astype(jnp.bfloat16)
    grad_field = cotangent.astype(jnp.float32) + conv_taps(
        pad_field(cotangent), conv_kernel, lat_dev, lon_dev, True
    )
    grad_rows = grad_field.reshape(mem_dev, cell_count, channels)
    grad_mixed = jnp.einsum(
        "mpc,dc->mpd",
        grad_rows.astype(jnp.bfloat16),
        output_weight,
        preferred_element_type=jnp.float32,
    )
    grad_mixed = grad_mixed.astype(jnp.bfloat16)
    grad_heads = split_heads(grad_mixed, HEAD_COUNT)
    dprob = jnp.einsum(
        "mphd,nphd->mnhp", grad_heads, value_heads, preferred_element_type=jnp.float32
    )
    dscore = (soft * (dprob - jnp.sum(soft * dprob, axis=1, keepdims=True))).astype(jnp.bfloat16)
    query_grad = (
        jnp.einsum("mnhp,nphd->mphd", dscore, key_heads, preferred_element_type=jnp.float32)
        * score_scale
    )
    query_grad = query_grad.reshape(query_raw.shape)
    row_count = mem_dev * lax.axis_size("member")
    key_part = (
        jnp.einsum("mnhp,mphd->nphd", dscore, query_heads, preferred_element_type=jnp.float32)
        * score_scale
    )
    value_part = jnp.einsum(
        "mnhp,mphd->nphd", rounded, grad_heads, preferred_element_type=jnp.float32
    )
    summed = lax.psum_scatter(
        jnp.concatenate(
            [
                key_part.reshape(row_count, cell_count, channels),
                value_part.reshape(row_count, cell_count, channels),
            ],
            axis=-1,
        ).astype(jnp.bfloat16),
        "member",
        scatter_dimension=0,
        tiled=True,
    ).astype(jnp.float32)
    key_grad = summed[..., :channels]
    value_grad = summed[..., channels:]
    grad_query_raw = head_pullback(query_raw, query_grad)
    grad_key_raw = head_pullback(key_raw, key_grad)
    grad_proj = jnp.concatenate([grad_query_raw, grad_key_raw, value_grad], axis=-1).astype(
        jnp.bfloat16
    )
    grad_normed = jnp.einsum(
        "mpe,ce->mpc", grad_proj, project_weight, preferred_element_type=jnp.float32
    )
    _, pull_norm = jax.vjp(lambda t: row_norm(t, norm_gain), inputs)
    grad_inputs = pull_norm(grad_normed)[0]
    grad_ensemble = (
        (grad_rows + grad_inputs).astype(jnp.bfloat16).reshape(mem_dev, lat_dev, lon_dev, channels)
    )
    return (result, grad_ensemble)


def solution(mesh):
    in_specs = (
        P("member", "lat", "lon", None),
        P(),
        P(),
        P(),
        P(),
        P("member", "lat", "lon", None),
    )
    out_specs = (P("member", "lat", "lon", None), P("member", "lat", "lon", None))
    return jax.shard_map(
        per_device, mesh=mesh, in_specs=in_specs, out_specs=out_specs, check_vma=False
    )
```

profile of v0, /device:TPU:1, one launch (start us, length us, event | category | flops | bytes accessed | tf_op | source)
XLA Modules:
  0.0 408.8 jit_solution(2294606689336277992)
XLA Ops:
  8.1 2.8 collective-permute-start.4
  20.1 4.0 collective-permute-start.7
  28.8 62.1 %all-gather.2.cloned.1.call-done = bf16[32,64,256]{2,1,0:T(8,128)(2,1)} async-done(((bf16[2,64,256]{2,1,0:T(8,128)(2,1)}), bf16[32,64,256]{2,1,0:T(8,128)(2,1)}) %all-gather.2.cloned.1.call-update) | async-done | bytes 1048592 | tf_op jit(solution)/shard_map/all_gather | solution.py:88
  98.1 6.5 %copy.153 = bf16[32,64,8,32]{3,0,1,2:T(8,128)(2,1)} copy(bf16[32,64,8,32]{1,3,2,0:T(8,128)(2,1)S(1)} %bitcast.179) | data formatting | bytes 2097152 | tf_op jit(solution)/shard_map/reshape | solution.py:39
  104.6 5.3 %fusion.115 = f32[8,64,32,2]{2,3,1,0:T(2,128)} fusion(bf16[32,64,8,32]{3,0,1,2:T(8,128)(2,1)} %copy.153, bf16[2,64,8,32]{3,0,1,2:T(2,128)(2,1)} %copy.154), kind=kOutput, calls=%fused_computation.175 | convolution fusion | flops 2097152 | bytes 1245184 | tf_op jit(solution)/shard_map/mphd,nphd->mnhp/dot_general | solution.py:133
  111.9 3.8 copy.139
  115.7 3.1 bitcast_reduce_fusion
  121.0 3.8 copy.140
  124.8 3.2 fusion
  130.8 7.5 %copy.145 = bf16[32,64,8,32]{3,0,1,2:T(8,128)(2,1)} copy(bf16[32,64,8,32]{1,3,2,0:T(8,128)(2,1)} %bitcast.181) | data formatting | bytes 2097152 | tf_op jit(solution)/shard_map/reshape | solution.py:39
  138.3 5.3 %fusion.114 = f32[8,64,32,2]{2,3,1,0:T(2,128)} fusion(bf16[32,64,8,32]{3,0,1,2:T(8,128)(2,1)} %copy.145, bf16[2,64,8,32]{3,0,1,2:T(2,128)(2,1)} %copy.146), kind=kOutput, calls=%fused_computation.174 | convolution fusion | flops 2097152 | bytes 1245184 | tf_op jit(solution)/shard_map/mphd,nphd->mnhp/dot_general | solution.py:103
  151.3 4.5 %multiply_convert_fusion = bf16[64,8,32,32]{3,2,1,0:T(8,128)(2,1)} fusion(bf16[2,64,8,32]{3,0,2,1:T(2,128)(2,1)} %copy.161, bf16[2,32,8,64]{1,0,2,3:T(2,128)(2,1)} %copy.157), kind=kOutput, calls=%fused_computation | convolution fusion | flops 3145728 | bytes 1179648 | tf_op jit(solution)/shard_map/mnhp,mphd->nphd/dot_general | solution.py:144
  155.8 4.9 %copy.167 = bf16[32,64,256]{2,1,0:T(8,128)(2,1)} copy(bf16[32,64,256]{0,2,1:T(8,128)(2,1)} %bitcast.183) | data formatting | bytes 2097152 | tf_op jit(solution)/shard_map/reshape | solution.py:153
  162.6 4.3 %convolution_convert_fusion = bf16[64,8,32,32]{3,2,1,0:T(8,128)(2,1)} fusion(bf16[2,64,8,32]{3,0,2,1:T(2,128)(2,1)} %copy.164, bf16[2,32,8,64]{1,0,2,3:T(2,128)(2,1)} %copy.149), kind=kOutput, calls=%fused_computation.2 | convolution fusion | flops 2621440 | bytes 1179648 | tf_op jit(solution)/shard_map/mnhp,mphd->nphd/dot_general | solution.py:147
  166.9 4.9 %copy.168 = bf16[32,64,256]{2,1,0:T(8,128)(2,1)} copy(bf16[32,64,256]{0,2,1:T(8,128)(2,1)} %bitcast.184) | data formatting | bytes 2097152 | tf_op jit(solution)/shard_map/reshape | solution.py:154
  171.8 3.1 pad_maximum_fusion
  174.9 7.8 %copy.156 = bf16[32,64,8,32]{3,0,2,1:T(8,128)(2,1)} copy(bf16[32,64,8,32]{1,3,2,0:T(8,128)(2,1)} %bitcast.182) | data formatting | bytes 2097152 | tf_op jit(solution)/shard_map/reshape | solution.py:39
  182.7 6.8 %copy.148 = bf16[32,64,8,32]{3,0,2,1:T(8,128)(2,1)} copy(bf16[32,64,8,32]{1,3,2,0:T(8,128)(2,1)S(1)} %bitcast.180) | data formatting | bytes 2097152 | tf_op jit(solution)/shard_map/reshape | solution.py:39
  189.5 3.4 fusion.116
  193.9 3.4 fusion.1
  197.5 182.2 %reduce-scatter.2.cloned.1.call-done = bf16[2,64,512]{2,1,0:T(8,128)(2,1)} async-done(((bf16[32,64,512]{2,1,0:T(8,128)(2,1)}), bf16[2,64,512]{2,1,0:T(8,128)(2,1)}) %reduce-scatter.2.cloned.1.call-update) | async-done | bytes 131088 | tf_op jit(solution)/shard_map/reduce_scatter | solution.py:150
  382.9 6.3 %collective-permute-start = (bf16[2,4,1,256]{3,2,1,0:T(2,128)(2,1)S(1)}, bf16[2,4,1,256]{3,2,1,0:T(2,128)(2,1)S(1)}, u32[]{:S(2)}, u32[]{:S(2)}) collective-permute-start(bf16[2,4,1,256]{3,2,1,0:T(2,128)(2,1)S(1)} %get-tuple-element.16), channel_id=1, source_target_pairs={{0,1},{1,2},{2,3},{3,0},{4,5},{5,6},{6,7},{7,4},{8,9},{9,10},{10,1... | collective-permute-start | bytes 12296 | tf_op jit(solution)/shard_map/ppermute | solution.py:19
  392.3 3.2 collective-permute-start.2
  397.0 3.1 collective-permute-done.3
  (119 shorter events, 49.0 us)
Async XLA Ops:
  7.2 19.4 %copy-start = (bf16[256,256]{1,0:T(8,128)(2,1)S(1)}, bf16[256,256]{1,0:T(8,128)(2,1)}, u32[]{:S(2)}) copy-start(bf16[256,256]{1,0:T(8,128)(2,1)} %param.9) | copy-start | bytes 393220
  7.2 11.6 %copy-start.5 = (bf16[2,4,16,256]{3,2,1,0:T(8,128)(2,1)S(1)}, bf16[2,4,16,256]{3,2,1,0:T(8,128)(2,1)}, u32[]{:S(2)}) copy-start(bf16[2,4,16,256]{3,2,1,0:T(8,128)(2,1)} %param.11) | copy-start | bytes 196612
  7.2 16.9 %copy-start.2 = (bf16[3,3,256,256]{3,2,1,0:T(8,128)(2,1)S(1)}, bf16[3,3,256,256]{3,2,1,0:T(8,128)(2,1)}, u32[]{:S(2)}) copy-start(bf16[3,3,256,256]{3,2,1,0:T(8,128)(2,1)} %param.10) | copy-start | bytes 3538948
  7.2 83.7 %all-gather.2.cloned.1.call-start = ((), (), s32[]{:S(2)}) async-start(), calls=%async_computation.1 | async-start | bytes 1114112 | tf_op jit(solution)/shard_map/all_gather | solution.py:88
  8.1 10.7 %collective-permute-start.4 = (bf16[2,4,1,256]{3,2,1,0:T(2,128)(2,1)S(1)}, bf16[2,4,1,256]{3,2,1,0:T(2,128)(2,1)S(1)}, u32[]{:S(2)}, u32[]{:S(2)}) collective-permute-start(bf16[2,4,1,256]{3,2,1,0:T(2,128)(2,1)S(1)} %get-tuple-element.18), channel_id=1, source_target_pairs={{0,1},{1,2},{2,3},{3,0},{4,5},{5,6},{6,7},{7,4},{8,9},{9,10},{10,1... | collective-permute-start | bytes 12296 | tf_op jit(solution)/shard_map/ppermute | solution.py:19
  10.9 7.9 %collective-permute-start.5 = (bf16[2,4,1,256]{3,2,1,0:T(2,128)(2,1)S(1)}, bf16[2,4,1,256]{3,2,1,0:T(2,128)(2,1)S(1)}, u32[]{:S(2)}, u32[]{:S(2)}) collective-permute-start(bf16[2,4,1,256]{3,2,1,0:T(2,128)(2,1)S(1)} %get-tuple-element.19), channel_id=1, source_target_pairs={{1,0},{2,1},{3,2},{0,3},{5,4},{6,5},{7,6},{4,7},{9,8},{10,9},{11,1... | collective-permute-start | bytes 12296 | tf_op jit(solution)/shard_map/ppermute | solution.py:22
  14.2 365.6 %reduce-scatter.2.cloned.1.call-start = ((), (), s32[]{:S(2)}) async-start(), calls=%async_computation.2 | async-start | bytes 2228224 | tf_op jit(solution)/shard_map/reduce_scatter | solution.py:150
  16.6 9.3 %copy-start.3 = (f32[2,64,256]{1,2,0:T(8,128)}, f32[2,64,256]{1,2,0:T(8,128)S(1)}, u32[]{:S(2)}) copy-start(f32[2,64,256]{1,2,0:T(8,128)S(1)} %copy.142) | copy-start | bytes 393220
  18.8 5.5 %collective-permute-start.6 = (bf16[2,1,18,256]{3,2,1,0:T(8,128)(2,1)S(1)}, bf16[2,1,18,256]{3,2,1,0:T(8,128)(2,1)S(1)}, u32[]{:S(2)}, u32[]{:S(2)}) collective-permute-start(bf16[2,1,18,256]{3,2,1,0:T(8,128)(2,1)S(1)} %get-tuple-element.14), channel_id=1, source_target_pairs={{4,0},{8,4},{12,8},{5,1},{9,5},{13,9},{6,2},{10,6},{14,10},{7,3},{... | collective-permute-start | bytes 55304 | tf_op jit(solution)/shard_map/ppermute | solution.py:22
  20.1 4.9 %collective-permute-start.7 = (bf16[2,1,18,256]{3,2,1,0:T(8,128)(2,1)S(1)}, bf16[2,1,18,256]{3,2,1,0:T(8,128)(2,1)S(1)}, u32[]{:S(2)}, u32[]{:S(2)}) collective-permute-start(bf16[2,1,18,256]{3,2,1,0:T(8,128)(2,1)S(1)} %get-tuple-element.15), channel_id=1, source_target_pairs={{0,4},{4,8},{8,12},{1,5},{5,9},{9,13},{2,6},{6,10},{10,14},{3,7},{... | collective-permute-start | bytes 55304 | tf_op jit(solution)/shard_map/ppermute | solution.py:19
  25.5 65.4 %copy-start.8 = (bf16[256,768]{1,0:T(8,128)(2,1)S(1)}, bf16[256,768]{1,0:T(8,128)(2,1)}, u32[]{:S(2)}) copy-start(bf16[256,768]{1,0:T(8,128)(2,1)} %param.8) | copy-start | bytes 1179652
  92.8 1.7 copy-start.1
  189.5 3.8 copy-start.4
  192.9 1.0 copy-start.6
  197.3 185.0 %copy-start.7 = (bf16[2,4,16,256]{3,2,1,0:T(8,128)(2,1)S(1)}, bf16[2,4,16,256]{3,2,1,0:T(8,128)(2,1)}, u32[]{:S(2)}) copy-start(bf16[2,4,16,256]{3,2,1,0:T(8,128)(2,1)} %param.6) | copy-start | bytes 196612
  197.3 185.0 %copy-start.9 = (bf16[256,768]{1,0:T(8,128)(2,1)S(1)}, bf16[256,768]{1,0:T(8,128)(2,1)}, u32[]{:S(2)}) copy-start(bf16[256,768]{1,0:T(8,128)(2,1)} %param.8) | copy-start | bytes 1179652
  197.3 185.0 %copy-start.11 = (f32[256]{0:T(256)S(1)}, f32[256]{0:T(256)}, u32[]{:S(2)}) copy-start(f32[256]{0:T(256)} %param.7) | copy-start | bytes 3076
  379.8 1.6 copy-start.10
  379.8 2.5 slice-start
  382.9 7.2 %collective-permute-start = (bf16[2,4,1,256]{3,2,1,0:T(2,128)(2,1)S(1)}, bf16[2,4,1,256]{3,2,1,0:T(2,128)(2,1)S(1)}, u32[]{:S(2)}, u32[]{:S(2)}) collective-permute-start(bf16[2,4,1,256]{3,2,1,0:T(2,128)(2,1)S(1)} %get-tuple-element.16), channel_id=1, source_target_pairs={{0,1},{1,2},{2,3},{3,0},{4,5},{5,6},{6,7},{7,4},{8,9},{9,10},{10,1... | collective-permute-start | bytes 12296 | tf_op jit(solution)/shard_map/ppermute | solution.py:19
  389.2 3.1 collective-permute-start.1
  392.3 4.7 %collective-permute-start.2 = (bf16[2,1,18,256]{3,2,1,0:T(8,128)(2,1)S(1)}, bf16[2,1,18,256]{3,2,1,0:T(8,128)(2,1)S(1)}, u32[]{:S(2)}, u32[]{:S(2)}) collective-permute-start(bf16[2,1,18,256]{3,2,1,0:T(8,128)(2,1)S(1)} %get-tuple-element.10), channel_id=1, source_target_pairs={{0,4},{4,8},{8,12},{1,5},{5,9},{9,13},{2,6},{6,10},{10,14},{3,7},{... | collective-permute-start | bytes 55304 | tf_op jit(solution)/shard_map/ppermute | solution.py:19
  395.5 4.6 %collective-permute-start.3 = (bf16[2,1,18,256]{3,2,1,0:T(8,128)(2,1)S(1)}, bf16[2,1,18,256]{3,2,1,0:T(8,128)(2,1)S(1)}, u32[]{:S(2)}, u32[]{:S(2)}) collective-permute-start(bf16[2,1,18,256]{3,2,1,0:T(8,128)(2,1)S(1)} %get-tuple-element.11), channel_id=1, source_target_pairs={{4,0},{8,4},{12,8},{5,1},{9,5},{13,9},{6,2},{10,6},{14,10},{7,3},{... | collective-permute-start | bytes 55304 | tf_op jit(solution)/shard_map/ppermute | solution.py:22
Sparse Core Ops, SparseCore 0:
  14.3 76.5 all-gather.1
  175.0 204.7 reduce-scatter.1
where the time goes:
time: 410 us; the launch traced here: 409 us
  waiting for transfers between devices  250 us (61%)
  local copies, waits for them, and re-layouts  69.1 us (17%)
  matrix products  34.8 us (8%)
  other arithmetic  20.5 us (5%)
  starting transfers between devices  19.5 us (5%)
  between operations  14.7 us (4%)
    reduce_scatter x1, waiting for transfers between devices, per_device(): lax.psum_scatter(jnp.concatenate([key_part.reshape(row_count, cell_count,...  182 us
    all_gather x1, waiting for transfers between devices, per_device(): lax.all_gather(normed, 'member', axis=0, tiled=True)  62.1 us
    reshape x8, local copies, waits for them, and re-layouts, split_heads(): values.reshape(values.shape[:-1] + (head_count, values.shape[-1] // head_...  32.2 us
    ppermute x4, starting transfers between devices, padded_2(): lax.ppermute(lax.slice_in_dim(block, block.shape[dim] - width, None, axis...  16.2 us
  transfers between devices with their start and end apart: 10, of which 5 were waited for; matrix products, arithmetic and copies ran while one was open for 8% of the time, Pallas kernels for 0%

commit v1 on v0

--- a/solution.py
+++ b/solution.py
@@ -7,6 +7,13 @@
 HEAD_COUNT = 8
 FLOOR = 0.5
 EPSILON = 1e-06
+
+
+def gather_over(x, name, d):
+    size = lax.axis_size(name)
+    tiles = jnp.stack([x for _ in range(size)])
+    tiles = lax.all_to_all(tiles, name, split_axis=0, concat_axis=0)
+    return jnp.concatenate(tiles, axis=d)
 
 
 def padded_2(block, sides, width, periodic):
@@ -85,7 +92,7 @@
         normed, project_weight[:, :channels], preferred_element_type=jnp.float32
     ).astype(jnp.bfloat16)
     gathered = jnp.dot(
-        lax.all_gather(normed, "member", axis=0, tiled=True),
+        gather_over(normed, "member", 0),
         project_weight[:, channels:],
         preferred_element_type=jnp.float32,
     ).astype(jnp.bfloat16)

time: 410 us -> 368 us (0.90)
  waiting for transfers between devices: 250 us -> 199 us
  starting transfers between devices: 19.5 us -> 29.4 us
    all_gather x1 -> x0, waiting for transfers between devices: 62.1 us -> none  [per_device(): lax.all_gather(normed, 'member', axis=0, tiled=True)]
    all_to_all x0 -> x1, waiting for transfers between devices: none -> 13 us  [gather_over(): tiles = lax.all_to_all(tiles, name, split_axis=0, concat_axis=0)]
    all_to_all x0 -> x1, starting transfers between devices: none -> 10 us  [gather_over(): tiles = lax.all_to_all(tiles, name, split_axis=0, concat_axis=0)]
  transfers between devices with their start and end apart: 10 -> 10, of which waited for: 5 -> 5; matrix products, arithmetic and copies ran while one was open for 8% -> 9% of each run, Pallas kernels for 0% -> 0%
where the time goes in v1:
time: 368 us; the launch traced here: 366 us
  waiting for transfers between devices  199 us (54%)
  local copies, waits for them, and re-layouts  70.1 us (19%)
  matrix products  33.5 us (9%)
  starting transfers between devices  29.4 us (8%)
  other arithmetic  19.8 us (5%)
  between operations  14.7 us (4%)
    reduce_scatter x1, waiting for transfers between devices, per_device(): lax.psum_scatter(jnp.concatenate([key_part.reshape(row_count, cell_count,...  180 us
    reshape x8, local copies, waits for them, and re-layouts, split_heads(): values.reshape(values.shape[:-1] + (head_count, values.shape[-1] // head_...  32.3 us
    ppermute x4, starting transfers between devices, padded_2(): lax.ppermute(lax.slice_in_dim(block, block.shape[dim] - width, None, axis...  16.1 us
    all_to_all x1, waiting for transfers between devices, gather_over(): tiles = lax.all_to_all(tiles, name, split_axis=0, concat_axis=0)  13 us
    all_to_all x1, starting transfers between devices, gather_over(): tiles = lax.all_to_all(tiles, name, split_axis=0, concat_axis=0)  10 us
  transfers between devices with their start and end apart: 10, of which 5 were waited for; matrix products, arithmetic and copies ran while one was open for 9% of the time, Pallas kernels for 0%

profile of v1, /device:TPU:1, one launch (start us, length us, event | category | flops | bytes accessed | tf_op | source)
XLA Modules:
  0.0 366.3 jit_solution(11104704746102220765)
XLA Ops:
  14.5 10.0 %all-to-all-start = ((bf16[16,2,64,256]{3,2,1,0:T(8,128)(2,1)}), bf16[16,2,64,256]{3,2,1,0:T(8,128)(2,1)S(1)}, u32[]{:S(2)}, u32[]{:S(2)}) async-start(bf16[16,2,64,256]{3,2,1,0:T(8,128)(2,1)} %stack.2), calls=%async_computation | async-start | bytes 2097152 | tf_op jit(solution)/shard_map/all_to_all | solution.py:15
  29.6 4.0 %collective-permute-start.7 = (bf16[2,1,18,256]{3,2,1,0:T(8,128)(2,1)S(1)}, bf16[2,1,18,256]{3,2,1,0:T(8,128)(2,1)S(1)}, u32[]{:S(2)}, u32[]{:S(2)}) collective-permute-start(bf16[2,1,18,256]{3,2,1,0:T(8,128)(2,1)S(1)} %get-tuple-element.15), channel_id=1, source_target_pairs={{0,4},{4,8},{8,12},{1,5},{5,9},{9,13},{2,6},{6,10},{10,14},{3,7},{... | collective-permute-start | bytes 55304 | tf_op jit(solution)/shard_map/ppermute | solution.py:26
  38.2 13.0 %all-to-all-done = bf16[16,2,64,256]{3,2,1,0:T(8,128)(2,1)S(1)} async-done(((bf16[16,2,64,256]{3,2,1,0:T(8,128)(2,1)}), bf16[16,2,64,256]{3,2,1,0:T(8,128)(2,1)S(1)}, u32[]{:S(2)}, u32[]{:S(2)}) %all-to-all-start) | async-done | bytes 1048608 | tf_op jit(solution)/shard_map/all_to_all | solution.py:15
  58.2 6.5 %copy.153 = bf16[32,64,8,32]{3,0,1,2:T(8,128)(2,1)} copy(bf16[32,64,8,32]{1,3,2,0:T(8,128)(2,1)S(1)} %bitcast.180) | data formatting | bytes 2097152 | tf_op jit(solution)/shard_map/reshape | solution.py:46
  64.6 5.3 %fusion.115 = f32[8,64,32,2]{2,3,1,0:T(2,128)} fusion(bf16[32,64,8,32]{3,0,1,2:T(8,128)(2,1)} %copy.153, bf16[2,64,8,32]{3,0,1,2:T(2,128)(2,1)} %copy.154), kind=kOutput, calls=%fused_computation.175 | convolution fusion | flops 2097152 | bytes 1245184 | tf_op jit(solution)/shard_map/mphd,nphd->mnhp/dot_general | solution.py:140
  71.9 3.8 %copy.139 = f32[32,64,256]{1,2,0:T(8,128)} copy(f32[32,64,256]{2,1,0:T(8,128)} %convert_multiply_fusion.1) | data formatting | bytes 4194304 | tf_op jit(solution)/shard_map/mul | solution.py:41
  75.7 3.1 bitcast_reduce_fusion
  81.0 3.8 %copy.140 = f32[32,64,256]{2,1,0:T(8,128)} copy(f32[32,64,256]{1,2,0:T(8,128)} %bitcast.186) | data formatting | bytes 4194304 | tf_op jit(solution)/shard_map/mul | solution.py:42
  84.9 3.2 fusion
  90.8 7.5 %copy.145 = bf16[32,64,8,32]{3,0,1,2:T(8,128)(2,1)} copy(bf16[32,64,8,32]{1,3,2,0:T(8,128)(2,1)} %bitcast.182) | data formatting | bytes 2097152 | tf_op jit(solution)/shard_map/reshape | solution.py:46
  98.3 5.3 %fusion.114 = f32[8,64,32,2]{2,3,1,0:T(2,128)} fusion(bf16[32,64,8,32]{3,0,1,2:T(8,128)(2,1)} %copy.145, bf16[2,64,8,32]{3,0,1,2:T(2,128)(2,1)} %copy.146), kind=kOutput, calls=%fused_computation.174 | convolution fusion | flops 2097152 | bytes 1245184 | tf_op jit(solution)/shard_map/mphd,nphd->mnhp/dot_general | solution.py:110
  111.4 4.5 %multiply_convert_fusion = bf16[64,8,32,32]{3,2,1,0:T(8,128)(2,1)} fusion(bf16[2,64,8,32]{3,0,2,1:T(2,128)(2,1)} %copy.161, bf16[2,32,8,64]{1,0,2,3:T(2,128)(2,1)} %copy.157), kind=kOutput, calls=%fused_computation | convolution fusion | flops 3145728 | bytes 1179648 | tf_op jit(solution)/shard_map/mnhp,mphd->nphd/dot_general | solution.py:151
  115.9 4.9 %copy.167 = bf16[32,64,256]{2,1,0:T(8,128)(2,1)} copy(bf16[32,64,256]{0,2,1:T(8,128)(2,1)} %bitcast.184) | data formatting | bytes 2097152 | tf_op jit(solution)/shard_map/reshape | solution.py:160
  122.6 4.3 %convolution_convert_fusion = bf16[64,8,32,32]{3,2,1,0:T(8,128)(2,1)} fusion(bf16[2,64,8,32]{3,0,2,1:T(2,128)(2,1)} %copy.164, bf16[2,32,8,64]{1,0,2,3:T(2,128)(2,1)} %copy.149), kind=kOutput, calls=%fused_computation.2 | convolution fusion | flops 2621440 | bytes 1179648 | tf_op jit(solution)/shard_map/mnhp,mphd->nphd/dot_general | solution.py:154
  126.9 4.9 %copy.168 = bf16[32,64,256]{2,1,0:T(8,128)(2,1)} copy(bf16[32,64,256]{0,2,1:T(8,128)(2,1)} %bitcast.185) | data formatting | bytes 2097152 | tf_op jit(solution)/shard_map/reshape | solution.py:161
  131.7 3.1 pad_maximum_fusion
  134.8 7.8 %copy.156 = bf16[32,64,8,32]{3,0,2,1:T(8,128)(2,1)} copy(bf16[32,64,8,32]{1,3,2,0:T(8,128)(2,1)} %bitcast.183) | data formatting | bytes 2097152 | tf_op jit(solution)/shard_map/reshape | solution.py:46
  142.6 6.8 %copy.148 = bf16[32,64,8,32]{3,0,2,1:T(8,128)(2,1)} copy(bf16[32,64,8,32]{1,3,2,0:T(8,128)(2,1)S(1)} %bitcast.181) | data formatting | bytes 2097152 | tf_op jit(solution)/shard_map/reshape | solution.py:46
  149.5 3.5 fusion.116
  153.9 3.4 fusion.1
  157.6 179.7 %reduce-scatter.2.cloned.1.call-done = bf16[2,64,512]{2,1,0:T(8,128)(2,1)} async-done(((bf16[32,64,512]{2,1,0:T(8,128)(2,1)}), bf16[2,64,512]{2,1,0:T(8,128)(2,1)}) %reduce-scatter.2.cloned.1.call-update) | async-done | bytes 131088 | tf_op jit(solution)/shard_map/reduce_scatter | solution.py:157
  340.4 6.3 %collective-permute-start = (bf16[2,4,1,256]{3,2,1,0:T(2,128)(2,1)S(1)}, bf16[2,4,1,256]{3,2,1,0:T(2,128)(2,1)S(1)}, u32[]{:S(2)}, u32[]{:S(2)}) collective-permute-start(bf16[2,4,1,256]{3,2,1,0:T(2,128)(2,1)S(1)} %get-tuple-element.16), channel_id=1, source_target_pairs={{0,1},{1,2},{2,3},{3,0},{4,5},{5,6},{6,7},{7,4},{8,9},{9,10},{10,1... | collective-permute-start | bytes 12296 | tf_op jit(solution)/shard_map/ppermute | solution.py:26
  349.8 3.1 collective-permute-start.2
  354.4 3.1 collective-permute-done.3
  (117 shorter events, 50.9 us)
Async XLA Ops:
  7.2 28.8 %copy-start = (bf16[256,256]{1,0:T(8,128)(2,1)S(1)}, bf16[256,256]{1,0:T(8,128)(2,1)}, u32[]{:S(2)}) copy-start(bf16[256,256]{1,0:T(8,128)(2,1)} %param.9) | copy-start | bytes 393220
  7.2 17.4 %copy-start.5 = (bf16[2,4,16,256]{3,2,1,0:T(8,128)(2,1)S(1)}, bf16[2,4,16,256]{3,2,1,0:T(8,128)(2,1)}, u32[]{:S(2)}) copy-start(bf16[2,4,16,256]{3,2,1,0:T(8,128)(2,1)} %param.11) | copy-start | bytes 196612
  7.2 17.4 %copy-start.2 = (bf16[3,3,256,256]{3,2,1,0:T(8,128)(2,1)S(1)}, bf16[3,3,256,256]{3,2,1,0:T(8,128)(2,1)}, u32[]{:S(2)}) copy-start(bf16[3,3,256,256]{3,2,1,0:T(8,128)(2,1)} %param.10) | copy-start | bytes 3538948
  8.1 20.1 %collective-permute-start.4 = (bf16[2,4,1,256]{3,2,1,0:T(2,128)(2,1)S(1)}, bf16[2,4,1,256]{3,2,1,0:T(2,128)(2,1)S(1)}, u32[]{:S(2)}, u32[]{:S(2)}) collective-permute-start(bf16[2,4,1,256]{3,2,1,0:T(2,128)(2,1)S(1)} %get-tuple-element.18), channel_id=1, source_target_pairs={{0,1},{1,2},{2,3},{3,0},{4,5},{5,6},{6,7},{7,4},{8,9},{9,10},{10,1... | collective-permute-start | bytes 12296 | tf_op jit(solution)/shard_map/ppermute | solution.py:26
  10.9 17.4 %collective-permute-start.5 = (bf16[2,4,1,256]{3,2,1,0:T(2,128)(2,1)S(1)}, bf16[2,4,1,256]{3,2,1,0:T(2,128)(2,1)S(1)}, u32[]{:S(2)}, u32[]{:S(2)}) collective-permute-start(bf16[2,4,1,256]{3,2,1,0:T(2,128)(2,1)S(1)} %get-tuple-element.19), channel_id=1, source_target_pairs={{1,0},{2,1},{3,2},{0,3},{5,4},{6,5},{7,6},{4,7},{9,8},{10,9},{11,1... | collective-permute-start | bytes 12296 | tf_op jit(solution)/shard_map/ppermute | solution.py:29
  14.5 36.7 %all-to-all-start = ((bf16[16,2,64,256]{3,2,1,0:T(8,128)(2,1)}), bf16[16,2,64,256]{3,2,1,0:T(8,128)(2,1)S(1)}, u32[]{:S(2)}, u32[]{:S(2)}) async-start(bf16[16,2,64,256]{3,2,1,0:T(8,128)(2,1)} %stack.2), calls=%async_computation | async-start | bytes 2097152 | tf_op jit(solution)/shard_map/all_to_all | solution.py:15
  24.6 312.7 %reduce-scatter.2.cloned.1.call-start = ((), (), s32[]{:S(2)}) async-start(), calls=%async_computation.2 | async-start | bytes 2228224 | tf_op jit(solution)/shard_map/reduce_scatter | solution.py:157
  26.0 9.3 %copy-start.3 = (f32[2,64,256]{1,2,0:T(8,128)}, f32[2,64,256]{1,2,0:T(8,128)S(1)}, u32[]{:S(2)}) copy-start(f32[2,64,256]{1,2,0:T(8,128)S(1)} %copy.142) | copy-start | bytes 393220
  28.3 5.5 %collective-permute-start.6 = (bf16[2,1,18,256]{3,2,1,0:T(8,128)(2,1)S(1)}, bf16[2,1,18,256]{3,2,1,0:T(8,128)(2,1)S(1)}, u32[]{:S(2)}, u32[]{:S(2)}) collective-permute-start(bf16[2,1,18,256]{3,2,1,0:T(8,128)(2,1)S(1)} %get-tuple-element.14), channel_id=1, source_target_pairs={{4,0},{8,4},{12,8},{5,1},{9,5},{13,9},{6,2},{10,6},{14,10},{7,3},{... | collective-permute-start | bytes 55304 | tf_op jit(solution)/shard_map/ppermute | solution.py:29
  29.6 4.9 %collective-permute-start.7 = (bf16[2,1,18,256]{3,2,1,0:T(8,128)(2,1)S(1)}, bf16[2,1,18,256]{3,2,1,0:T(8,128)(2,1)S(1)}, u32[]{:S(2)}, u32[]{:S(2)}) collective-permute-start(bf16[2,1,18,256]{3,2,1,0:T(8,128)(2,1)S(1)} %get-tuple-element.15), channel_id=1, source_target_pairs={{0,4},{4,8},{8,12},{1,5},{5,9},{9,13},{2,6},{6,10},{10,14},{3,7},{... | collective-permute-start | bytes 55304 | tf_op jit(solution)/shard_map/ppermute | solution.py:26
  52.9 1.7 copy-start.1
  149.5 3.8 %copy-start.4 = (f32[2,64,256]{1,2,0:T(8,128)S(1)}, f32[2,64,256]{1,2,0:T(8,128)}, u32[]{:S(2)}) copy-start(f32[2,64,256]{1,2,0:T(8,128)} %copy-done.3) | copy-start | bytes 393220
  152.9 1.0 copy-start.6
  157.3 182.5 %copy-start.7 = (bf16[2,4,16,256]{3,2,1,0:T(8,128)(2,1)S(1)}, bf16[2,4,16,256]{3,2,1,0:T(8,128)(2,1)}, u32[]{:S(2)}) copy-start(bf16[2,4,16,256]{3,2,1,0:T(8,128)(2,1)} %param.6) | copy-start | bytes 196612
  157.3 182.5 %copy-start.8 = (bf16[256,768]{1,0:T(8,128)(2,1)S(1)}, bf16[256,768]{1,0:T(8,128)(2,1)}, u32[]{:S(2)}) copy-start(bf16[256,768]{1,0:T(8,128)(2,1)} %param.8) | copy-start | bytes 1179652
  157.3 182.5 %copy-start.10 = (f32[256]{0:T(256)S(1)}, f32[256]{0:T(256)}, u32[]{:S(2)}) copy-start(f32[256]{0:T(256)} %param.7) | copy-start | bytes 3076
  337.3 1.6 copy-start.9
  337.3 2.5 slice-start
  340.4 7.2 %collective-permute-start = (bf16[2,4,1,256]{3,2,1,0:T(2,128)(2,1)S(1)}, bf16[2,4,1,256]{3,2,1,0:T(2,128)(2,1)S(1)}, u32[]{:S(2)}, u32[]{:S(2)}) collective-permute-start(bf16[2,4,1,256]{3,2,1,0:T(2,128)(2,1)S(1)} %get-tuple-element.16), channel_id=1, source_target_pairs={{0,1},{1,2},{2,3},{3,0},{4,5},{5,6},{6,7},{7,4},{8,9},{9,10},{10,1... | collective-permute-start | bytes 12296 | tf_op jit(solution)/shard_map/ppermute | solution.py:26
  346.7 3.1 collective-permute-start.1
  349.8 4.6 %collective-permute-start.2 = (bf16[2,1,18,256]{3,2,1,0:T(8,128)(2,1)S(1)}, bf16[2,1,18,256]{3,2,1,0:T(8,128)(2,1)S(1)}, u32[]{:S(2)}, u32[]{:S(2)}) collective-permute-start(bf16[2,1,18,256]{3,2,1,0:T(8,128)(2,1)S(1)} %get-tuple-element.10), channel_id=1, source_target_pairs={{0,4},{4,8},{8,12},{1,5},{5,9},{9,13},{2,6},{6,10},{10,14},{3,7},{... | collective-permute-start | bytes 55304 | tf_op jit(solution)/shard_map/ppermute | solution.py:26
  352.9 4.6 %collective-permute-start.3 = (bf16[2,1,18,256]{3,2,1,0:T(8,128)(2,1)S(1)}, bf16[2,1,18,256]{3,2,1,0:T(8,128)(2,1)S(1)}, u32[]{:S(2)}, u32[]{:S(2)}) collective-permute-start(bf16[2,1,18,256]{3,2,1,0:T(8,128)(2,1)S(1)} %get-tuple-element.11), channel_id=1, source_target_pairs={{4,0},{8,4},{12,8},{5,1},{9,5},{13,9},{6,2},{10,6},{14,10},{7,3},{... | collective-permute-start | bytes 55304 | tf_op jit(solution)/shard_map/ppermute | solution.py:29
Sparse Core Ops, SparseCore 0:
  135.0 202.2 reduce-scatter.1
